TPU v7x, 32 devices: a whole 2x2x4 slice. The times are simulated.
32 devices in a mesh: groups: 2 (over y), span: 4 (over z), head: 4 (over x, core).
Axes of the slice: x: 2, y: 2, z: 4, core: 2. Of those that a mesh axis runs over, the one named last changes fastest.
Arguments:
- query_rows: bfloat16 [2048, 6144], P(('groups', 'span', 'head')), parts along dimension 0, may hold values from -6 to 6
- key_rows: bfloat16 [2048, 1024], P(('groups', 'span', 'head')), parts along dimension 0, may hold values from -6 to 6
- value_rows: bfloat16 [2048, 1024], P(('groups', 'span', 'head')), parts along dimension 0, may hold values from -6 to 6
- frame_counts: int32 [16], P('groups'), parts along dimension 0, may hold values from 1 to 4, as said below
- noise_levels: int32 [16], P('groups'), parts along dimension 0, may hold values from 0 to 63
- span_mask: int32 [16, 8], P('groups'), parts along dimension 0, may hold values from 0 to 1, as said below
- level_gate: bfloat16 [64, 6144], P(None, 'head'), may hold values from 0.19921875 to 1.796875
Outputs:
- attended: bfloat16 [2048, 6144], P(('groups', 'span', 'head')), parts along dimension 0
There are 2 independent parts, one for each index of `groups`. A program takes and returns all parts, laid end to end along the dimension named above; an argument that names none is the same for every part. Nothing has to cross between parts.
Inputs may be any that keep to these rules, and one draw needn't show every extreme that they name: `frame_counts`: each span holds at least one frame, and some span holds exactly 4. span_mask[c, c] = 1 for every span, span_mask[c, e] = 0 for e > c, entries below the diagonal are 0 or 1.
All inputs are finite; a program needn't handle non-finite values.
Results may differ from a plain program's by a relative error of at most 0.0033.
Values may be sent and summed in bfloat16 or wider, within the bound.
No kernel may reach another device: no remote copies, remote signals or barrier semaphores. Data moves between devices by JAX's collectives and lax.ppermute only.
A program may use at most 64 MiB of HBM per device.

v0:
```python
import math
import jax
import jax.numpy as jnp
from jax import lax
from jax.sharding import PartitionSpec as P

HD = 128
FRAME_TOK = 32
CT = 128
CH_DEV = 2


def attend(slot_state, query_block, key_piece, value_piece, usable, score_scale):
    run_max, run_sum, run_acc = slot_state
    scores = (
        jnp.einsum("qhgd,khd->hgqk", query_block, key_piece, preferred_element_type=jnp.float32)
        * score_scale
    )
    scores = jnp.where(usable[None, None, None, :], scores, -jnp.inf)
    new_max = jnp.maximum(run_max, jnp.max(scores, axis=3))
    weights = jnp.exp(scores - new_max[..., None])
    factor = jnp.exp(run_max - new_max)
    new_sum = factor * run_sum + jnp.sum(weights, axis=3)
    update = jnp.einsum(
        "hgqk,khd->qhgd",
        weights.astype(jnp.bfloat16),
        value_piece,
        preferred_element_type=jnp.float32,
    )
    new_acc = run_acc * jnp.transpose(factor, (2, 0, 1))[..., None] + update
    return (new_max, new_sum, new_acc)


def body(query_rows, key_rows, value_rows, frame_counts, noise_levels, span_mask, level_gate):
    q_local, k_local, v_local = (
        lax.all_to_all(query_rows, "head", split_axis=1, concat_axis=0, tiled=True),
        lax.all_to_all(key_rows, "head", split_axis=1, concat_axis=0, tiled=True),
        lax.all_to_all(value_rows, "head", split_axis=1, concat_axis=0, tiled=True),
    )
    span_devices = lax.axis_size("span")
    device_index = lax.axis_index("span")
    heads_dev = q_local.shape[1] // HD
    kv_dev = k_local.shape[1] // HD
    group_size = heads_dev // kv_dev
    score_scale = 1.0 / math.sqrt(HD)
    first_block = q_local[:CT]
    second_block = q_local[CT:]
    own_spans = jnp.stack([2 * device_index, 2 * device_index + 1])
    total_rows = CH_DEV * span_devices * CT
    position = jnp.arange(CT, dtype=jnp.int32)
    live_rows = position[None, :] < (frame_counts * FRAME_TOK)[:, None]
    live_flat = live_rows.reshape(-1)
    queries = jnp.stack([first_block, second_block]).reshape(2, CT, kv_dev, group_size, HD)
    allowed = []
    query_live = []
    gate_rows = []
    for member in range(2):
        mask_row = lax.dynamic_index_in_dim(span_mask, own_spans[member], 0, keepdims=False)
        allowed.append((jnp.repeat(mask_row, CT, total_repeat_length=total_rows) > 0) & live_flat)
        query_live.append(lax.dynamic_index_in_dim(live_rows, own_spans[member], 0, keepdims=False))
        level_index = lax.dynamic_index_in_dim(noise_levels, own_spans[member], 0, keepdims=False)
        gate_rows.append(
            lax.dynamic_index_in_dim(level_gate, level_index, 0, keepdims=False).astype(jnp.float32)
        )
    allowed = jnp.stack(allowed)

    def fold_step(running, kv_piece):
        key_piece, value_piece = kv_piece
        piece_rows = key_piece.shape[0]
        key_piece = key_piece.reshape(piece_rows, kv_dev, HD)
        value_piece = value_piece.reshape(piece_rows, kv_dev, HD)
        usable = lax.slice_in_dim(allowed, 0, piece_rows, axis=1)
        results = []
        for member in range(2):
            slot_state = (running[0][member], running[1][member], running[2][member])

            def compute(slot_state, member=member):
                return attend(
                    slot_state, queries[member], key_piece, value_piece, usable[member], score_scale
                )

            def keep_state(slot_state):
                return slot_state

            results.append(lax.cond(jnp.any(usable[member]), compute, keep_state, slot_state))
        return (
            jnp.stack([results[0][0], results[1][0]]),
            jnp.stack([results[0][1], results[1][1]]),
            jnp.stack([results[0][2], results[1][2]]),
        )

    initial = (
        jnp.full((2, kv_dev, group_size, CT), -1e30, jnp.float32),
        jnp.zeros((2, kv_dev, group_size, CT), jnp.float32),
        jnp.zeros((2, CT, kv_dev, group_size, HD), jnp.float32),
    )
    run_max, run_sum, run_acc = fold_step(
        initial,
        (
            lax.all_gather(k_local, "span", axis=0, tiled=True),
            lax.all_gather(v_local, "span", axis=0, tiled=True),
        ),
    )
    outputs = []
    for member in range(2):
        normed = run_acc[member] / jnp.transpose(run_sum[member], (2, 0, 1))[..., None]
        normed = normed.reshape(CT, heads_dev * HD) * gate_rows[member][None, :]
        outputs.append(
            jnp.where(query_live[member][:, None], normed, jnp.float32(0.0)).astype(jnp.bfloat16)
        )
    first_out = outputs[0]
    second_out = outputs[1]
    merged = jnp.concatenate([first_out, second_out], axis=0)
    return lax.all_to_all(merged, "head", split_axis=0, concat_axis=1, tiled=True)


def solution(mesh):
    placed = (
        P(("groups", "span", "head"), None),
        P(("groups", "span", "head"), None),
        P(("groups", "span", "head"), None),
        P("groups"),
        P("groups"),
        P("groups", None),
        P(None, "head"),
    )
    return jax.shard_map(
        body,
        mesh=mesh,
        in_specs=placed,
        out_specs=P(("groups", "span", "head"), None),
        check_vma=False,
    )
```

profile of v0, /device:TPU:0, one launch (start us, length us, event | category | flops | bytes accessed | tf_op | source)
XLA Modules:
  0.0 101.1 jit_solution(4558437299421896229)
XLA Ops:
  0.0 1.6 %copy.85 = bf16[8,4,8,256]{3,2,0,1:T(8,128)(2,1)} copy(bf16[8,4,8,256]{3,2,1,0:T(8,128)(2,1)} %bitcast.212) | data formatting | bytes 262144 | tf_op jit(solution)/shard_map/all_to_all | solution.py:37
  1.6 4.2 %all-to-all-start.1 = ((bf16[64,4,256]{2,0,1:T(8,128)(2,1)}), bf16[64,4,256]{2,0,1:T(8,128)(2,1)S(1)}, u32[]{:S(2)}, u32[]{:S(2)}) async-start(bf16[64,4,256]{2,0,1:T(8,128)(2,1)} %bitcast.201), calls=%async_computation.1 | async-start | bytes 262144 | tf_op jit(solution)/shard_map/all_to_all | solution.py:37
  5.8 0.7 broadcast_multiply_fusion
  6.5 1.5 %copy.84 = bf16[8,4,8,256]{3,2,0,1:T(8,128)(2,1)} copy(bf16[8,4,8,256]{3,2,1,0:T(8,128)(2,1)} %bitcast.213) | data formatting | bytes 262144 | tf_op jit(solution)/shard_map/all_to_all | solution.py:38
  8.0 0.8 fusion.52
  8.8 0.7 fusion.57
  9.5 0.9 all-to-all-done.1
  10.4 3.3 %all-to-all-start.2 = ((bf16[64,4,256]{2,0,1:T(8,128)(2,1)}), bf16[64,4,256]{2,0,1:T(8,128)(2,1)S(1)}, u32[]{:S(2)}, u32[]{:S(2)}) async-start(bf16[64,4,256]{2,0,1:T(8,128)(2,1)} %bitcast.200), calls=%async_computation.2 | async-start | bytes 262144 | tf_op jit(solution)/shard_map/all_to_all | solution.py:38
  13.7 10.7 %fusion.54 = (pred[]{:T(512)}, pred[1024]{0:T(1024)(128)(4,1)S(1)}, pred[]{:T(512)}, pred[1024]{0:T(1024)(128)(4,1)S(1)}) fusion(s32[8]{0:T(128)S(1)} %broadcast_multiply_fusion, s32[]{:T(128)} %bitcast.22, s32[]{:T(128)} %bitcast.21, s32[]{:T(128)} %bitcast.20, s32[]{:T(128)} %bitcast.19, s32[]{:T(128)} %bitcast.18, s32[]{:T(128)} %bitcast.17, s32[]{:T(128)} %bitcast.16, ...), kind=kLoop, calls=%fused_computation.79 | loop fusion | flops 38910 | bytes 2146 | tf_op jit(solution)/shard_map/reduce_or | solution.py:85
  24.4 2.1 %copy.83 = bf16[8,4,8,1536]{3,2,0,1:T(8,128)(2,1)} copy(bf16[8,4,8,1536]{3,2,1,0:T(8,128)(2,1)} %bitcast.207) | data formatting | bytes 1572864 | tf_op jit(solution)/shard_map/all_to_all | solution.py:36
  26.5 3.5 %all-to-all-start = ((bf16[64,4,1536]{2,0,1:T(8,128)(2,1)}), bf16[64,4,1536]{2,0,1:T(8,128)(2,1)S(1)}, u32[]{:S(2)}, u32[]{:S(2)}) async-start(bf16[64,4,1536]{2,0,1:T(8,128)(2,1)} %bitcast.199), calls=%async_computation | async-start | bytes 1572864 | tf_op jit(solution)/shard_map/all_to_all | solution.py:36
  30.1 1.4 %fusion.58 = (s32[1]{0:T(128)}, s32[1]{0:T(128)}) fusion(s32[8]{0:T(128)} %param.21, s32[]{:T(128)S(6)} %select_n.53, s32[]{:T(128)S(6)} %select_n.50), kind=kLoop, calls=%fused_computation.83 | loop fusion | bytes 24 | tf_op jit(solution)/shard_map/jit(dynamic_index_in_dim)/dynamic_slice | solution.py:61
  36.5 0.8 convert_reduce_fusion.1
  37.3 17.0 %all_gather.7 = bf16[1024,256]{1,0:T(8,128)(2,1)S(1)} all-gather(bf16[256,256]{1,0:T(8,128)(2,1)S(1)} %bitcast.209), channel_id=1, replica_groups=mesh['groups'=2,'span'=4,'head'=4] {'span'}, dimensions={0}, use_global_device_ids=true | all-gather | bytes 655360 | tf_op jit(solution)/shard_map/all_gather | solution.py:101
  54.3 1.0 copy.47
  55.3 16.0 %all_gather.6 = bf16[1024,256]{1,0:T(8,128)(2,1)S(1)} all-gather(bf16[256,256]{1,0:T(8,128)(2,1)S(1)} %bitcast.208), channel_id=1, replica_groups=mesh['groups'=2,'span'=4,'head'=4] {'span'}, dimensions={0}, use_global_device_ids=true | all-gather | bytes 655360 | tf_op jit(solution)/shard_map/all_gather | solution.py:100
  71.6 0.5 stack.10
  72.1 0.5 stack.9
  72.7 5.9 %conditional.2 = (f32[2,6,128]{2,1,0:T(8,128)S(1)}, f32[128,2,6,128]{0,3,2,1:T(8,128)S(1)}) conditional(s32[]{:T(128)} %convert_element_type.22, () %tuple.29, (pred[1024]{0:T(1024)(128)(4,1)S(1)}, bf16[2,128,2,6,128]{4,3,2,1,0:T(8,128)(2,1)S(1)}, bf16[1024,2,128]{0,2,1:T(8,128)(2,1)S(1)}, bf16[1024,2,128]{0,2,1:T(8,128)(2,1)}) %tuple.84), branch_computations={%region_1.3_spmd, %region_2.6_spmd} | conditional | flops 822809088 | bytes 26416172 | solution.py:85
  73.0 1.5 %bitcast_reduce_fusion = (f32[2,6,128]{2,1,0:T(8,128)S(1)}, f32[2,1024,128,6]{2,1,3,0:T(8,128)S(1)}) fusion(pred[1024]{0:T(1024)(128)(4,1)S(1)} %get-tuple-element.42, bf16[2,128,2,6,128]{4,1,3,2,0:T(8,128)(2,1)S(1)} %copy.48, bf16[1024,2,128]{0,2,1:T(8,128)(2,1)S(1)} %get-tuple-element.76), kind=kOutput, calls=%fused_computation.1 | convolution fusion | flops 407370240 | bytes 7216128 | tf_op jit(solution)/shard_map/cond/branch_1_fun/qhgd,khd->hgqk/dot_general | solution.py:16
  74.5 1.8 %fusion.2 = f32[2,6,128]{2,1,0:T(8,128)S(1)} fusion(f32[2,1024,128,6]{2,1,3,0:T(8,128)S(1)} %get-tuple-element.93, f32[2,6,128]{2,1,0:T(8,128)S(1)} %broadcast_maximum_fusion, pred[1024]{0:T(1024)(128)(4,1)S(1)} %get-tuple-element.42), kind=kLoop, calls=%fused_computation.5 | loop fusion | flops 6289920 | bytes 6304768 | tf_op jit(solution)/shard_map/cond/branch_1_fun/reduce_sum | solution.py:23
  76.3 2.1 %fusion.9 = f32[128,2,6,128]{3,0,2,1:T(8,128)S(1)} fusion(f32[2,1024,128,6]{2,1,3,0:T(8,128)S(1)} %get-tuple-element.93, f32[2,6,128]{2,1,0:T(8,128)S(1)} %broadcast_maximum_fusion, pred[1024]{0:T(1024)(128)(4,1)S(1)} %get-tuple-element.42, bf16[1024,2,128]{0,2,1:T(8,128)(2,1)S(1)} %copy-done, f32[128,2,6]{0,2,1:T(8,128)S(1)} %get-tuple-element.90), kind=kOutput, calls=%fused_computation.9 | convolution fusion | flops 409141248 | bytes 7615488 | tf_op jit(solution)/shard_map/cond/branch_1_fun/hgqk,khd->qhgd/dot_general | solution.py:24
  78.3 0.3 copy.73
  78.7 6.0 %conditional.3 = (f32[2,6,128]{2,1,0:T(8,128)S(1)}, f32[128,2,6,128]{0,3,2,1:T(8,128)S(1)}) conditional(s32[]{:T(128)} %convert_element_type.24, () %tuple.31, (pred[1024]{0:T(1024)(128)(4,1)S(1)}, bf16[2,128,2,6,128]{4,3,2,1,0:T(8,128)(2,1)S(1)}, bf16[1024,2,128]{0,2,1:T(8,128)(2,1)S(1)}, bf16[1024,2,128]{0,2,1:T(8,128)(2,1)}) %tuple.85), branch_computations={%region_6.8_spmd, %region_7.11_spmd} | conditional | flops 822809088 | bytes 26416172 | solution.py:85
  79.1 1.5 %bitcast_reduce_fusion.1 = (f32[2,6,128]{2,1,0:T(8,128)S(1)}, f32[2,1024,128,6]{2,1,3,0:T(8,128)S(1)}) fusion(pred[1024]{0:T(1024)(128)(4,1)S(1)} %get-tuple-element.46, bf16[2,128,2,6,128]{4,1,3,2,0:T(8,128)(2,1)S(1)} %copy.52, bf16[1024,2,128]{0,2,1:T(8,128)(2,1)S(1)} %get-tuple-element.80), kind=kOutput, calls=%fused_computation.21 | convolution fusion | flops 407370240 | bytes 7216128 | tf_op jit(solution)/shard_map/cond/branch_1_fun/qhgd,khd->hgqk/dot_general | solution.py:16
  80.6 1.8 %fusion.21 = f32[2,6,128]{2,1,0:T(8,128)S(1)} fusion(f32[2,1024,128,6]{2,1,3,0:T(8,128)S(1)} %get-tuple-element.97, f32[2,6,128]{2,1,0:T(8,128)S(1)} %broadcast_maximum_fusion.1, pred[1024]{0:T(1024)(128)(4,1)S(1)} %get-tuple-element.46), kind=kLoop, calls=%fused_computation.25 | loop fusion | flops 6289920 | bytes 6304768 | tf_op jit(solution)/shard_map/cond/branch_1_fun/reduce_sum | solution.py:23
  82.4 2.1 %fusion.28 = f32[128,2,6,128]{3,0,2,1:T(8,128)S(1)} fusion(f32[2,1024,128,6]{2,1,3,0:T(8,128)S(1)} %get-tuple-element.97, f32[2,6,128]{2,1,0:T(8,128)S(1)} %broadcast_maximum_fusion.1, pred[1024]{0:T(1024)(128)(4,1)S(1)} %get-tuple-element.46, bf16[1024,2,128]{0,2,1:T(8,128)(2,1)S(1)} %copy-done.1, f32[128,2,6]{0,2,1:T(8,128)S(1)} %get-tuple-element.94), kind=kOutput, calls=%fused_computation.29 | convolution fusion | flops 409141248 | bytes 7615488 | tf_op jit(solution)/shard_map/cond/branch_1_fun/hgqk,khd->qhgd/dot_general | solution.py:24
  84.8 0.3 fusion.41
  85.1 0.3 fusion.39
  85.5 0.3 copy.56
  85.7 14.4 %all_to_all.73 = bf16[4,64,1536]{2,1,0:T(8,128)(2,1)S(1)} all-to-all(bf16[4,64,1536]{2,1,0:T(8,128)(2,1)S(1)} %bitcast.205), channel_id=1, replica_groups=mesh['groups'=2,'span'=4,'head'=4] {'head'}, dimensions={0} | all-to-all | bytes 1572864 | tf_op jit(solution)/shard_map/all_to_all | solution.py:114
  100.1 0.9 copy.79
  (22 shorter events, 1.5 us)
Async XLA Ops:
  1.6 8.8 %all-to-all-start.1 = ((bf16[64,4,256]{2,0,1:T(8,128)(2,1)}), bf16[64,4,256]{2,0,1:T(8,128)(2,1)S(1)}, u32[]{:S(2)}, u32[]{:S(2)}) async-start(bf16[64,4,256]{2,0,1:T(8,128)(2,1)} %bitcast.201), calls=%async_computation.1 | async-start | bytes 262144 | tf_op jit(solution)/shard_map/all_to_all | solution.py:37
  10.4 16.1 %all-to-all-start.2 = ((bf16[64,4,256]{2,0,1:T(8,128)(2,1)}), bf16[64,4,256]{2,0,1:T(8,128)(2,1)S(1)}, u32[]{:S(2)}, u32[]{:S(2)}) async-start(bf16[64,4,256]{2,0,1:T(8,128)(2,1)} %bitcast.200), calls=%async_computation.2 | async-start | bytes 262144 | tf_op jit(solution)/shard_map/all_to_all | solution.py:38
  26.5 45.0 %all-to-all-start = ((bf16[64,4,1536]{2,0,1:T(8,128)(2,1)}), bf16[64,4,1536]{2,0,1:T(8,128)(2,1)S(1)}, u32[]{:S(2)}, u32[]{:S(2)}) async-start(bf16[64,4,1536]{2,0,1:T(8,128)(2,1)} %bitcast.199), calls=%async_computation | async-start | bytes 1572864 | tf_op jit(solution)/shard_map/all_to_all | solution.py:36
  73.0 3.3 %copy-start = (bf16[1024,2,128]{0,2,1:T(8,128)(2,1)S(1)}, bf16[1024,2,128]{0,2,1:T(8,128)(2,1)}, u32[]{:S(2)}) copy-start(bf16[1024,2,128]{0,2,1:T(8,128)(2,1)} %get-tuple-element.77) | copy-start | bytes 1572868 | tf_op jit(solution)/shard_map/cond
  79.1 3.3 %copy-start.1 = (bf16[1024,2,128]{0,2,1:T(8,128)(2,1)S(1)}, bf16[1024,2,128]{0,2,1:T(8,128)(2,1)}, u32[]{:S(2)}) copy-start(bf16[1024,2,128]{0,2,1:T(8,128)(2,1)} %get-tuple-element.81) | copy-start | bytes 1572868 | tf_op jit(solution)/shard_map/cond
where the time goes:
time: 102 us; the launch traced here: 101 us
  blocking collectives  47.4 us (46%)
  other arithmetic  16.6 us (16%)
  local copies, waits for them, and re-layouts  12.6 us (12%)
  starting transfers between devices  11.1 us (11%)
  matrix products  7.04 us (7%)
  between operations  5.14 us (5%)
    all_gather x1, blocking collectives, body(): lax.all_gather(v_local, 'span', axis=0, tiled=True)  17 us
    all_gather x1, blocking collectives, body(): lax.all_gather(k_local, 'span', axis=0, tiled=True)  16 us
    all_to_all x1, blocking collectives, body(): lax.all_to_all(merged, 'head', split_axis=0, concat_axis=1, tiled=True)  14.4 us
    reduce_or x1, other arithmetic, fold_step(): jnp.any(usable[member])  10.7 us
    all_to_all x1, starting transfers between devices, body(): lax.all_to_all(key_rows, 'head', split_axis=1, concat_axis=0, tiled=True)  4.24 us
    dot_general x2, matrix products, attend(): jnp.einsum('hgqk,khd->qhgd', weights.astype(jnp.bfloat16), value_piece, p...  4.1 us
    reduce_sum x2, other arithmetic, attend(): new_sum = factor * run_sum + jnp.sum(weights, axis=3)  3.54 us
    all_to_all x1, starting transfers between devices, body(): lax.all_to_all(query_rows, 'head', split_axis=1, concat_axis=0, tiled=True)  3.5 us
  transfers between devices with their start and end apart: 3, of which 1 were waited for; matrix products, arithmetic and copies ran while one was open for 20% of the time, Pallas kernels for 0%

commit v1 on v0

--- a/solution.py
+++ b/solution.py
@@ -34,7 +34,12 @@
 def body(query_rows, key_rows, value_rows, frame_counts, noise_levels, span_mask, level_gate):
     q_local, k_local, v_local = (
         lax.all_to_all(query_rows, "head", split_axis=1, concat_axis=0, tiled=True),
-        lax.all_to_all(key_rows, "head", split_axis=1, concat_axis=0, tiled=True),
+        jnp.concatenate(
+            lax.all_to_all(
+                jnp.stack(jnp.split(key_rows, lax.axis_size("head"), axis=1)), "head", 0, 0
+            ),
+            axis=0,
+        ),
         lax.all_to_all(value_rows, "head", split_axis=1, concat_axis=0, tiled=True),
     )
     span_devices = lax.axis_size("span")

time: 102 us -> 102 us (level)
    all_to_all x1 -> x0, local copies, waits for them, and re-layouts: 1.57 us -> none  [body(): lax.all_to_all(key_rows, 'head', split_axis=1, concat_axis=0, tiled=True)]
where the time goes in v1:
time: 102 us; the launch traced here: 101 us
  blocking collectives  47.4 us (46%)
  other arithmetic  17.3 us (17%)
  local copies, waits for them, and re-layouts  11.9 us (12%)
  starting transfers between devices  11.1 us (11%)
  matrix products  7.03 us (7%)
  between operations  5.04 us (5%)
    all_gather x1, blocking collectives, body(): lax.all_gather(k_local, 'span', axis=0, tiled=True)  17 us
    all_gather x1, blocking collectives, body(): lax.all_gather(v_local, 'span', axis=0, tiled=True)  16 us
    all_to_all x1, blocking collectives, body(): lax.all_to_all(merged, 'head', split_axis=0, concat_axis=1, tiled=True)  14.4 us
    reduce_or x1, other arithmetic, fold_step(): jnp.any(usable[member])  10.8 us
    all_to_all x1, starting transfers between devices, body(): lax.all_to_all(value_rows, 'head', split_axis=1, concat_axis=0, tiled=True)  4.24 us
    dot_general x2, matrix products, attend(): jnp.einsum('hgqk,khd->qhgd', weights.astype(jnp.bfloat16), value_piece, p...  4.1 us
    reduce_sum x2, other arithmetic, attend(): new_sum = factor * run_sum + jnp.sum(weights, axis=3)  3.54 us
    all_to_all x1, starting transfers between devices, body(): lax.all_to_all(query_rows, 'head', split_axis=1, concat_axis=0, tiled=True)  3.5 us
  transfers between devices with their start and end apart: 3, of which 1 were waited for; matrix products, arithmetic and copies ran while one was open for 20% of the time, Pallas kernels for 0%

profile of v1, /device:TPU:0, one launch (start us, length us, event | category | flops | bytes accessed | tf_op | source)
XLA Modules:
  0.0 101.0 jit_solution(2970483900391583913)
XLA Ops:
  0.0 1.6 %copy.80 = bf16[8,4,8,256]{3,2,0,1:T(8,128)(2,1)} copy(bf16[8,4,8,256]{3,2,1,0:T(8,128)(2,1)} %bitcast.214) | data formatting | bytes 262144 | tf_op jit(solution)/shard_map/all_to_all | solution.py:43
  1.6 4.2 %all-to-all-start.2 = ((bf16[64,4,256]{2,0,1:T(8,128)(2,1)}), bf16[64,4,256]{2,0,1:T(8,128)(2,1)S(1)}, u32[]{:S(2)}, u32[]{:S(2)}) async-start(bf16[64,4,256]{2,0,1:T(8,128)(2,1)} %bitcast.203), calls=%async_computation.2 | async-start | bytes 262144 | tf_op jit(solution)/shard_map/all_to_all | solution.py:43
  5.8 0.7 broadcast_multiply_fusion
  6.5 0.8 slice_bitcast_fusion.7
  7.3 0.8 fusion.52
  8.1 0.7 pad_maximum_fusion.1
  8.7 0.7 fusion.57
  9.4 1.0 all-to-all-done.2
  10.4 3.3 %all-to-all-start.1 = ((bf16[4,64,256]{2,1,0:T(8,128)(2,1)}), bf16[4,64,256]{2,1,0:T(8,128)(2,1)S(1)}, u32[]{:S(2)}, u32[]{:S(2)}) async-start(bf16[4,64,256]{2,1,0:T(8,128)(2,1)} %pad_maximum_fusion.1), calls=%async_computation.1 | async-start | bytes 262144 | tf_op jit(solution)/shard_map/all_to_all | solution.py:38
  13.7 10.8 %fusion.54 = (pred[]{:T(512)}, pred[1024]{0:T(1024)(128)(4,1)S(1)}, pred[]{:T(512)}, pred[1024]{0:T(1024)(128)(4,1)S(1)}) fusion(s32[8]{0:T(128)S(1)} %broadcast_multiply_fusion, s32[]{:T(128)} %bitcast.22, s32[]{:T(128)} %bitcast.21, s32[]{:T(128)} %bitcast.20, s32[]{:T(128)} %bitcast.19, s32[]{:T(128)} %bitcast.18, s32[]{:T(128)} %bitcast.17, s32[]{:T(128)} %bitcast.16, ...), kind=kLoop, calls=%fused_computation.83 | loop fusion | flops 38910 | bytes 2146 | tf_op jit(solution)/shard_map/reduce_or | solution.py:90
  24.5 2.1 %copy.79 = bf16[8,4,8,1536]{3,2,0,1:T(8,128)(2,1)} copy(bf16[8,4,8,1536]{3,2,1,0:T(8,128)(2,1)} %bitcast.209) | data formatting | bytes 1572864 | tf_op jit(solution)/shard_map/all_to_all | solution.py:36
  26.6 3.5 %all-to-all-start = ((bf16[64,4,1536]{2,0,1:T(8,128)(2,1)}), bf16[64,4,1536]{2,0,1:T(8,128)(2,1)S(1)}, u32[]{:S(2)}, u32[]{:S(2)}) async-start(bf16[64,4,1536]{2,0,1:T(8,128)(2,1)} %bitcast.202), calls=%async_computation | async-start | bytes 1572864 | tf_op jit(solution)/shard_map/all_to_all | solution.py:36
  30.1 1.3 %fusion.58 = (s32[1]{0:T(128)}, s32[1]{0:T(128)}) fusion(s32[8]{0:T(128)} %param.21, s32[]{:T(128)S(6)} %select_n.53, s32[]{:T(128)S(6)} %select_n.50), kind=kLoop, calls=%fused_computation.87 | loop fusion | bytes 24 | tf_op jit(solution)/shard_map/jit(dynamic_index_in_dim)/dynamic_slice | solution.py:66
  36.4 0.8 convert_reduce_fusion.1
  37.2 17.0 %all_gather.6 = bf16[1024,256]{1,0:T(8,128)(2,1)S(1)} all-gather(bf16[256,256]{1,0:T(8,128)(2,1)S(1)} %bitcast.211), channel_id=1, replica_groups=mesh['groups'=2,'span'=4,'head'=4] {'span'}, dimensions={0}, use_global_device_ids=true | all-gather | bytes 655360 | tf_op jit(solution)/shard_map/all_gather | solution.py:105
  54.4 16.0 %all_gather.7 = bf16[1024,256]{1,0:T(8,128)(2,1)S(1)} all-gather(bf16[256,256]{1,0:T(8,128)(2,1)S(1)} %bitcast.210), channel_id=1, replica_groups=mesh['groups'=2,'span'=4,'head'=4] {'span'}, dimensions={0}, use_global_device_ids=true | all-gather | bytes 655360 | tf_op jit(solution)/shard_map/all_gather | solution.py:106
  70.4 1.0 copy.45
  71.5 0.5 stack.25
  72.0 0.5 stack.24
  72.7 5.9 %conditional.2 = (f32[2,6,128]{2,1,0:T(8,128)S(1)}, f32[128,2,6,128]{0,3,2,1:T(8,128)S(1)}) conditional(s32[]{:T(128)} %convert_element_type.22, () %tuple.29, (pred[1024]{0:T(1024)(128)(4,1)S(1)}, bf16[2,128,2,6,128]{4,3,2,1,0:T(8,128)(2,1)S(1)}, bf16[1024,2,128]{0,2,1:T(8,128)(2,1)S(1)}, bf16[1024,2,128]{0,2,1:T(8,128)(2,1)}) %tuple.87), branch_computations={%region_1.3_spmd, %region_2.6_spmd} | conditional | flops 822809088 | bytes 26416172 | solution.py:90
  72.9 1.5 %bitcast_reduce_fusion = (f32[2,6,128]{2,1,0:T(8,128)S(1)}, f32[2,1024,128,6]{2,1,3,0:T(8,128)S(1)}) fusion(pred[1024]{0:T(1024)(128)(4,1)S(1)} %get-tuple-element.42, bf16[2,128,2,6,128]{4,1,3,2,0:T(8,128)(2,1)S(1)} %copy.46, bf16[1024,2,128]{0,2,1:T(8,128)(2,1)S(1)} %get-tuple-element.76), kind=kOutput, calls=%fused_computation.1 | convolution fusion | flops 407370240 | bytes 7216128 | tf_op jit(solution)/shard_map/cond/branch_1_fun/qhgd,khd->hgqk/dot_general | solution.py:16
  74.4 1.8 %fusion.2 = f32[2,6,128]{2,1,0:T(8,128)S(1)} fusion(f32[2,1024,128,6]{2,1,3,0:T(8,128)S(1)} %get-tuple-element.93, f32[2,6,128]{2,1,0:T(8,128)S(1)} %broadcast_maximum_fusion, pred[1024]{0:T(1024)(128)(4,1)S(1)} %get-tuple-element.42), kind=kLoop, calls=%fused_computation.5 | loop fusion | flops 6289920 | bytes 6304768 | tf_op jit(solution)/shard_map/cond/branch_1_fun/reduce_sum | solution.py:23
  76.2 2.0 %fusion.9 = f32[128,2,6,128]{3,0,2,1:T(8,128)S(1)} fusion(f32[2,1024,128,6]{2,1,3,0:T(8,128)S(1)} %get-tuple-element.93, f32[2,6,128]{2,1,0:T(8,128)S(1)} %broadcast_maximum_fusion, pred[1024]{0:T(1024)(128)(4,1)S(1)} %get-tuple-element.42, bf16[1024,2,128]{0,2,1:T(8,128)(2,1)S(1)} %copy-done, f32[128,2,6]{0,2,1:T(8,128)S(1)} %get-tuple-element.90), kind=kOutput, calls=%fused_computation.9 | convolution fusion | flops 409141248 | bytes 7615488 | tf_op jit(solution)/shard_map/cond/branch_1_fun/hgqk,khd->qhgd/dot_general | solution.py:24
  78.6 6.0 %conditional.3 = (f32[2,6,128]{2,1,0:T(8,128)S(1)}, f32[128,2,6,128]{0,3,2,1:T(8,128)S(1)}) conditional(s32[]{:T(128)} %convert_element_type.24, () %tuple.31, (pred[1024]{0:T(1024)(128)(4,1)S(1)}, bf16[2,128,2,6,128]{4,3,2,1,0:T(8,128)(2,1)S(1)}, bf16[1024,2,128]{0,2,1:T(8,128)(2,1)S(1)}, bf16[1024,2,128]{0,2,1:T(8,128)(2,1)}) %tuple.88), branch_computations={%region_6.8_spmd, %region_7.11_spmd} | conditional | flops 822809088 | bytes 26416172 | solution.py:90
  79.0 1.5 %bitcast_reduce_fusion.1 = (f32[2,6,128]{2,1,0:T(8,128)S(1)}, f32[2,1024,128,6]{2,1,3,0:T(8,128)S(1)}) fusion(pred[1024]{0:T(1024)(128)(4,1)S(1)} %get-tuple-element.46, bf16[2,128,2,6,128]{4,1,3,2,0:T(8,128)(2,1)S(1)} %copy.50, bf16[1024,2,128]{0,2,1:T(8,128)(2,1)S(1)} %get-tuple-element.80), kind=kOutput, calls=%fused_computation.21 | convolution fusion | flops 407370240 | bytes 7216128 | tf_op jit(solution)/shard_map/cond/branch_1_fun/qhgd,khd->hgqk/dot_general | solution.py:16
  80.5 1.8 %fusion.21 = f32[2,6,128]{2,1,0:T(8,128)S(1)} fusion(f32[2,1024,128,6]{2,1,3,0:T(8,128)S(1)} %get-tuple-element.97, f32[2,6,128]{2,1,0:T(8,128)S(1)} %broadcast_maximum_fusion.1, pred[1024]{0:T(1024)(128)(4,1)S(1)} %get-tuple-element.46), kind=kLoop, calls=%fused_computation.25 | loop fusion | flops 6289920 | bytes 6304768 | tf_op jit(solution)/shard_map/cond/branch_1_fun/reduce_sum | solution.py:23
  82.3 2.1 %fusion.28 = f32[128,2,6,128]{3,0,2,1:T(8,128)S(1)} fusion(f32[2,1024,128,6]{2,1,3,0:T(8,128)S(1)} %get-tuple-element.97, f32[2,6,128]{2,1,0:T(8,128)S(1)} %broadcast_maximum_fusion.1, pred[1024]{0:T(1024)(128)(4,1)S(1)} %get-tuple-element.46, bf16[1024,2,128]{0,2,1:T(8,128)(2,1)S(1)} %copy-done.1, f32[128,2,6]{0,2,1:T(8,128)S(1)} %get-tuple-element.94), kind=kOutput, calls=%fused_computation.29 | convolution fusion | flops 409141248 | bytes 7615488 | tf_op jit(solution)/shard_map/cond/branch_1_fun/hgqk,khd->qhgd/dot_general | solution.py:24
  84.7 0.3 fusion.41
  85.0 0.3 fusion.39
  85.4 0.3 copy.54
  85.6 14.4 %all_to_all.59 = bf16[4,64,1536]{2,1,0:T(8,128)(2,1)S(1)} all-to-all(bf16[4,64,1536]{2,1,0:T(8,128)(2,1)S(1)} %bitcast.207), channel_id=1, replica_groups=mesh['groups'=2,'span'=4,'head'=4] {'head'}, dimensions={0} | all-to-all | bytes 1572864 | tf_op jit(solution)/shard_map/all_to_all | solution.py:119
  100.1 0.9 copy.76
  (23 shorter events, 1.8 us)
Async XLA Ops:
  1.6 8.8 %all-to-all-start.2 = ((bf16[64,4,256]{2,0,1:T(8,128)(2,1)}), bf16[64,4,256]{2,0,1:T(8,128)(2,1)S(1)}, u32[]{:S(2)}, u32[]{:S(2)}) async-start(bf16[64,4,256]{2,0,1:T(8,128)(2,1)} %bitcast.203), calls=%async_computation.2 | async-start | bytes 262144 | tf_op jit(solution)/shard_map/all_to_all | solution.py:43
  10.4 16.2 %all-to-all-start.1 = ((bf16[4,64,256]{2,1,0:T(8,128)(2,1)}), bf16[4,64,256]{2,1,0:T(8,128)(2,1)S(1)}, u32[]{:S(2)}, u32[]{:S(2)}) async-start(bf16[4,64,256]{2,1,0:T(8,128)(2,1)} %pad_maximum_fusion.1), calls=%async_computation.1 | async-start | bytes 262144 | tf_op jit(solution)/shard_map/all_to_all | solution.py:38
  26.6 44.9 %all-to-all-start = ((bf16[64,4,1536]{2,0,1:T(8,128)(2,1)}), bf16[64,4,1536]{2,0,1:T(8,128)(2,1)S(1)}, u32[]{:S(2)}, u32[]{:S(2)}) async-start(bf16[64,4,1536]{2,0,1:T(8,128)(2,1)} %bitcast.202), calls=%async_computation | async-start | bytes 1572864 | tf_op jit(solution)/shard_map/all_to_all | solution.py:36
  72.9 3.3 %copy-start = (bf16[1024,2,128]{0,2,1:T(8,128)(2,1)S(1)}, bf16[1024,2,128]{0,2,1:T(8,128)(2,1)}, u32[]{:S(2)}) copy-start(bf16[1024,2,128]{0,2,1:T(8,128)(2,1)} %get-tuple-element.77) | copy-start | bytes 1572868 | tf_op jit(solution)/shard_map/cond
  79.0 3.3 %copy-start.1 = (bf16[1024,2,128]{0,2,1:T(8,128)(2,1)S(1)}, bf16[1024,2,128]{0,2,1:T(8,128)(2,1)}, u32[]{:S(2)}) copy-start(bf16[1024,2,128]{0,2,1:T(8,128)(2,1)} %get-tuple-element.81) | copy-start | bytes 1572868 | tf_op jit(solution)/shard_map/cond
